TPU v7x, 256 devices: a whole 4x4x8 slice. The times are simulated.
256 devices in a mesh: sub: 64 (over x, z, core), slab: 4 (over y).
Axes of the slice: x: 4, y: 4, z: 8, core: 2. Of those that a mesh axis runs over, the one named last changes fastest.
Arguments:
- adjoint_load: float32 [4, 64, 2, 4, 3200], P('slab', 'sub')
- design: float32 [4, 64, 2032], P('slab', 'sub'), may hold values from 0 to 1
- viscous_block: float32 [24, 24], replicated
- brinkman_block: float32 [24, 24], replicated
- coupling: float32 [8, 24], replicated, may hold values from -1.2 to 1.2
- stabilization: float32 [8, 8], replicated
- neighbours: int32 [4, 64, 3], P('slab', 'sub'), may hold values from -1 to 63, as said below
- iface_nodes: int32 [4, 64, 3, 256], P('slab', 'sub'), may hold values from 0 to 3199, as said below
- iface_count: int32 [4, 64, 3], P('slab', 'sub'), may hold values from 0 to 256, as said below
- face_nodes: int32 [4, 64, 2, 512], P('slab', 'sub'), may hold values from 0 to 3199, as said below
- owner_ids: int32 [4, 64, 3, 256], P('slab', 'sub'), may hold values from 0 to 63, as said below
Outputs:
- solution: float32 [4, 64, 2, 4, 3200], P('slab', 'sub')
- coefficients: float32 [2, 3], replicated
Inputs may be any that keep to these rules, and one draw needn't show every extreme that they name: In round r the neighbour of subdomain i is i XOR 2^r or -1 for none; two neighbours list each other. `iface_nodes`: per subdomain, all entries here and in face_nodes are distinct local nodes. Slot k of round r names the same physical node on a subdomain and on its round-r neighbour; only the first iface_count slots are shared. `iface_count`: equal on both sides of a pair, 0 where the round has no neighbour. `face_nodes`: face 0 is the lower face, face 1 the upper one; slot k of the upper face of slab s is slot k of the lower face of slab s + 1 at the same index along sub. `owner_ids`: for a used slot, one of the two subdomains of the pair, the same on both sides; for an unused slot, the subdomain's own index.
All inputs are finite; a program needn't handle non-finite values.
Results may differ from a plain program's by a relative error of at most 0.0003.
Values sent between devices are 32-bit elements; how exact they have to be, the bound alone decides.
No kernel may reach another device: no remote copies, remote signals or barrier semaphores. Data moves between devices by JAX's collectives and lax.ppermute only.
A program may use at most 128 MiB of HBM per device.

v0:
```python
import jax
import jax.numpy as jnp
from jax import lax
from jax.sharding import PartitionSpec as P

EX = 4
EY = 4
EZ = 127
IFACE = 256
ROUNDS = 3
KRYLOV = 3
CASES = 2
ELEMS = 2032
NODES = 3200
PRECISE = lax.Precision.HIGHEST
BRINKMAN_MAX = 4.0
RAMP_PARAM = 0.1


def swapped(block, axis, bit):
    count = lax.axis_size(axis)
    route = []
    for low in range(count):
        high = low | 1 << bit
        if high != low and high < count:
            route += [(low, high), (high, low)]
    return lax.ppermute(block, axis, route)


def extended_2(block, sides, width):
    for axis, dim in sides:
        count = lax.axis_size(axis)
        forward = [(i, i + 1) for i in range(count - 1)]
        backward = [(target, source) for source, target in forward]
        low = lax.ppermute(
            lax.slice_in_dim(block, block.shape[dim] - width, None, axis=dim), axis, forward
        )
        high = lax.ppermute(lax.slice_in_dim(block, 0, width, axis=dim), axis, backward)
        block = jnp.concatenate([low, block, high], axis=dim)
    return block


def corner_offsets(corner):
    return (corner // 4, corner // 2 % 2, corner % 2)


def element_vectors(field):
    channels = field.shape[0]
    node_grid = field.reshape(channels, EX + 1, EY + 1, EZ + 1)
    corner_list = []
    for corner in range(8):
        shift_x, shift_y, shift_z = corner_offsets(corner)
        window = node_grid[
            :, shift_x : shift_x + EX, shift_y : shift_y + EY, shift_z : shift_z + EZ
        ]
        corner_list.append(window.reshape(channels, ELEMS))
    return jnp.stack(corner_list, axis=1)


def node_sums(element_out):
    channels = element_out.shape[0]
    summed = jnp.zeros((channels, EX + 1, EY + 1, EZ + 1), jnp.float32)
    for corner in range(8):
        shift_x, shift_y, shift_z = corner_offsets(corner)
        corner_block = element_out[:, corner].reshape(channels, EX, EY, EZ)
        summed = summed + jnp.pad(
            corner_block,
            ((0, 0), (shift_x, 1 - shift_x), (shift_y, 1 - shift_y), (shift_z, 1 - shift_z)),
        )
    return summed.reshape(channels, NODES)


def brinkman_of(design):
    return BRINKMAN_MAX * RAMP_PARAM * (1.0 - design) / (RAMP_PARAM + design)


def adjoint_terms(state, brinkman, viscous_block, brinkman_block, coupling, stabilization):
    values = element_vectors(state).reshape(CASES, 32, ELEMS)
    velocity = values[:, :24]
    pressure = values[:, 24:]
    out_velocity = jnp.einsum("ij,cie->cje", viscous_block, velocity, precision=PRECISE)
    out_velocity = out_velocity + brinkman * jnp.einsum(
        "ij,cie->cje", brinkman_block, velocity, precision=PRECISE
    )
    out_velocity = out_velocity + jnp.einsum("kj,cke->cje", coupling, pressure, precision=PRECISE)
    out_pressure = jnp.einsum("kj,cje->cke", coupling, velocity, precision=PRECISE) - jnp.einsum(
        "lk,cle->cke", stabilization, pressure, precision=PRECISE
    )
    element_out = jnp.concatenate([out_velocity, out_pressure], axis=1).reshape(CASES * 4, 8, ELEMS)
    return node_sums(element_out)


def divergence_terms(velocity_nodes, coupling):
    element_vel = element_vectors(velocity_nodes).reshape(CASES, 24, ELEMS)
    return node_sums(jnp.einsum("kj,cje->cke", coupling, element_vel, precision=PRECISE))


def gradient_terms(pressure_nodes, coupling):
    element_pre = element_vectors(pressure_nodes)
    element_out = jnp.einsum("kj,cke->cje", coupling, element_pre, precision=PRECISE).reshape(
        CASES * 3, 8, ELEMS
    )
    return node_sums(element_out)


def diagonal_terms(brinkman, viscous_block, brinkman_block):
    diag_elem = (
        jnp.diagonal(viscous_block)[:, None]
        + jnp.diagonal(brinkman_block)[:, None] * brinkman[None, :]
    )
    return node_sums(diag_elem.reshape(3, 8, ELEMS))


def schur_terms(diag_nodes, coupling, stabilization):
    inverse = 1.0 / element_vectors(diag_nodes).reshape(24, ELEMS)
    schur_elem = (
        jnp.einsum("kj,je->ke", coupling * coupling, inverse, precision=PRECISE)
        + jnp.diagonal(stabilization)[:, None]
    )
    return node_sums(schur_elem[None])


def node_weights(iface_nodes, not_owned, lower_face, lower_lost):
    weights = jnp.ones((NODES,), jnp.float32)
    for matching in range(ROUNDS):
        keep = jnp.where(not_owned[matching], 0.0, 1.0).astype(weights.dtype)
        weights = weights.at[iface_nodes[matching]].multiply(keep)
    return weights.at[lower_face].multiply(jnp.where(lower_lost, 0.0, 1.0).astype(weights.dtype))


def assemble(partial_sums, layout):
    iface_nodes, iface_count, neighbours, face_nodes = layout
    slot_ids = jnp.arange(IFACE, dtype=jnp.int32)
    slot_valid = (slot_ids[None, :] < iface_count[:, None]).astype(jnp.float32)
    outgoing = jnp.stack(
        [
            partial_sums[:, iface_nodes[matching]] * slot_valid[matching][None, :]
            for matching in range(ROUNDS)
        ]
    )
    present = (neighbours >= 0).astype(jnp.float32)
    incoming = jnp.stack(
        [swapped(outgoing[matching], "sub", matching) for matching in range(ROUNDS)]
    )
    incoming = incoming * present[:, None, None]
    face_out = jnp.stack([partial_sums[:, face_nodes[0]], partial_sums[:, face_nodes[1]]])
    extended = extended_2(face_out, (("slab", 0),), 1)
    summed = partial_sums
    for matching in range(ROUNDS):
        summed = summed.at[:, iface_nodes[matching]].add(incoming[matching])
    summed = summed.at[:, face_nodes[0]].add(extended[0])
    return summed.at[:, face_nodes[1]].add(extended[3])


def weighted_norms(vectors, weights):
    return lax.psum(jnp.sum(weights * vectors * vectors, axis=(1, 2)), ("sub", "slab"))


def triangular_solves(factor, target):
    middle = []
    for row_index in range(KRYLOV):
        remainder = target[:, row_index] - sum(
            (factor[:, row_index, col_index] * middle[col_index] for col_index in range(row_index))
        )
        middle.append(remainder / factor[:, row_index, row_index])
    result = [None] * KRYLOV
    for row_index in reversed(range(KRYLOV)):
        remainder = middle[row_index] - sum(
            (
                factor[:, col_index, row_index] * result[col_index]
                for col_index in range(row_index + 1, KRYLOV)
            )
        )
        result[row_index] = remainder / factor[:, row_index, row_index]
    return jnp.stack(result, axis=1)


def per_device(
    adjoint_load,
    design,
    viscous_block,
    brinkman_block,
    coupling,
    stabilization,
    neighbours,
    iface_nodes,
    iface_count,
    face_nodes,
    owner_ids,
):
    layout = (iface_nodes[0, 0], iface_count[0, 0], neighbours[0, 0], face_nodes[0, 0])
    brinkman = brinkman_of(design[0, 0])
    sub_index = lax.axis_index("sub")
    slab_index = lax.axis_index("slab")
    slot_ids = jnp.arange(IFACE, dtype=jnp.int32)
    not_owned = (slot_ids[None, :] < iface_count[0, 0][:, None]) & (owner_ids[0, 0] != sub_index)
    weights = node_weights(iface_nodes[0, 0], not_owned, face_nodes[0, 0, 0], slab_index > 0)
    owned_load = (adjoint_load[0, 0] * weights).reshape(CASES * 4, NODES)
    assembled = assemble(
        jnp.concatenate(
            [owned_load, diagonal_terms(brinkman, viscous_block, brinkman_block)], axis=0
        ),
        layout,
    )
    start_vec = assembled[: CASES * 4].reshape(CASES, 4, NODES)
    diag_nodes = assembled[CASES * 4 :]
    schur_diag = assemble(schur_terms(diag_nodes, coupling, stabilization), layout)[0]
    start_norm = jnp.sqrt(weighted_norms(start_vec, weights))
    krylov_basis = [start_vec / start_norm[:, None, None]]
    hessenberg = jnp.zeros((CASES, KRYLOV + 1, KRYLOV), jnp.float32)
    directions = []
    for krylov_step in range(KRYLOV):
        precondition_vector = krylov_basis[-1]
        velocity_guess = precondition_vector[:, :3] / diag_nodes[None]
        divergence = assemble(
            divergence_terms(velocity_guess.reshape(CASES * 3, NODES), coupling), layout
        )
        pressure = (divergence - precondition_vector[:, 3]) / schur_diag[None]
        gradient = assemble(gradient_terms(pressure, coupling), layout).reshape(CASES, 3, NODES)
        velocity = velocity_guess - gradient / diag_nodes[None]
        direction = jnp.concatenate([velocity, pressure[:, None]], axis=1)
        directions.append(direction)
        image_part = adjoint_terms(
            direction.reshape(CASES * 4, NODES),
            brinkman,
            viscous_block,
            brinkman_block,
            coupling,
            stabilization,
        )
        product_vec = assemble(image_part, layout).reshape(CASES, 4, NODES)
        local_heights = jnp.stack(
            [jnp.sum(weights * vector * product_vec, axis=(1, 2)) for vector in krylov_basis],
            axis=1,
        )
        heights = lax.psum(local_heights, ("sub", "slab"))
        for basis_index in range(len(krylov_basis)):
            product_vec = (
                product_vec - heights[:, basis_index, None, None] * krylov_basis[basis_index]
            )
        length = jnp.sqrt(weighted_norms(product_vec, weights))
        hessenberg = hessenberg.at[:, : krylov_step + 1, krylov_step].set(heights)
        hessenberg = hessenberg.at[:, krylov_step + 1, krylov_step].set(length)
        krylov_basis.append(product_vec / length[:, None, None])
    normal_matrix = jnp.einsum("cij,cik->cjk", hessenberg, hessenberg, precision=PRECISE)
    target = start_norm[:, None] * hessenberg[:, 0, :]
    factor = jnp.linalg.cholesky(normal_matrix)
    coefficients = triangular_solves(factor, target)
    solution = sum(
        (
            coefficients[:, krylov_step, None, None] * directions[krylov_step]
            for krylov_step in range(KRYLOV)
        )
    )
    return (solution[None, None], coefficients)


def solution(mesh):
    placed = (
        P("slab", "sub", None, None, None),
        P("slab", "sub", None),
        P(),
        P(),
        P(),
        P(),
        P("slab", "sub", None),
        P("slab", "sub", None, None),
        P("slab", "sub", None),
        P("slab", "sub", None, None),
        P("slab", "sub", None, None),
    )
    return jax.shard_map(
        per_device,
        mesh=mesh,
        in_specs=placed,
        out_specs=(P("slab", "sub", None, None, None), P()),
        check_vma=False,
    )
```

profile of v0, /device:TPU:1, one launch (start us, length us, event | category | flops | bytes accessed | tf_op | source)
XLA Modules:
  0.0 1081.2 jit_solution(7967894446121106461)
XLA Ops:
  52.0 79.0 %psum.49 = f32[2]{0:T(128)S(1)} all-reduce(f32[2]{0:T(128)S(1)} %reduce_sum.120), channel_id=1, replica_groups=mesh['sub'=64,'slab'=4] {'sub','slab'}, use_global_device_ids=true, to_apply=%region_11.12 | all-reduce | flops 2 | bytes 16 | tf_op jit(solution)/shard_map/psum | solution.py:156
  211.3 4.1 scatter_custom_fusion.12
  247.5 4.3 collective-permute-start.18
  261.6 4.0 scatter_custom_fusion.22
  265.7 4.2 scatter_custom_fusion.23
  288.6 4.0 pad_add_fusion.4
  302.9 4.3 collective-permute-start.23
  326.1 75.0 %psum.50 = f32[2,1]{0,1:T(1,128)S(1)} all-reduce(f32[2,1]{0,1:T(1,128)S(1)} %bitcast.877), channel_id=1, replica_groups=mesh['sub'=64,'slab'=4] {'sub','slab'}, use_global_device_ids=true, to_apply=%region_34.35 | all-reduce | flops 2 | bytes 16 | tf_op jit(solution)/shard_map/psum | solution.py:236
  401.7 74.1 %psum.51 = f32[2]{0:T(128)S(1)} all-reduce(f32[2]{0:T(128)S(1)} %reduce_sum.129), channel_id=1, replica_groups=mesh['sub'=64,'slab'=4] {'sub','slab'}, use_global_device_ids=true, to_apply=%region_37.38 | all-reduce | flops 2 | bytes 16 | tf_op jit(solution)/shard_map/psum | solution.py:156
  502.8 4.2 scatter_custom_fusion.32
  540.7 4.3 collective-permute-start.33
  558.9 4.4 scatter_custom_fusion.38
  582.0 4.0 pad_add_fusion.2
  596.0 4.3 collective-permute-start.38
  620.4 74.9 %psum.52 = f32[2,2]{0,1:T(2,128)S(1)} all-reduce(f32[2,2]{0,1:T(2,128)S(1)} %pad_maximum_fusion.8), channel_id=1, replica_groups=mesh['sub'=64,'slab'=4] {'sub','slab'}, use_global_device_ids=true, to_apply=%region_57.58 | all-reduce | flops 4 | bytes 32 | tf_op jit(solution)/shard_map/psum | solution.py:236
  696.2 74.0 %psum.53 = f32[2]{0:T(128)S(1)} all-reduce(f32[2]{0:T(128)S(1)} %reduce_sum.144), channel_id=1, replica_groups=mesh['sub'=64,'slab'=4] {'sub','slab'}, use_global_device_ids=true, to_apply=%region_60.61 | all-reduce | flops 2 | bytes 16 | tf_op jit(solution)/shard_map/psum | solution.py:156
  800.4 4.4 scatter_custom_fusion.47
  823.7 4.1 pad_add_fusion.1
  837.8 4.3 collective-permute-start.48
  857.4 4.3 scatter_custom_fusion.53
  880.4 4.0 pad_add_fusion
  898.0 4.3 collective-permute-start.53
  924.5 74.4 %psum.54 = f32[2,3]{0,1:T(4,128)S(1)} all-reduce(f32[2,3]{0,1:T(4,128)S(1)} %pad_maximum_fusion.7), channel_id=1, replica_groups=mesh['sub'=64,'slab'=4] {'sub','slab'}, use_global_device_ids=true, to_apply=%region_83.84 | all-reduce | flops 6 | bytes 48 | tf_op jit(solution)/shard_map/psum | solution.py:236
  1003.1 74.3 %psum.55 = f32[2]{0:T(128)S(1)} all-reduce(f32[2]{0:T(128)S(1)} %reduce_sum.189), channel_id=1, replica_groups=mesh['sub'=64,'slab'=4] {'sub','slab'}, use_global_device_ids=true, to_apply=%region_86.87 | all-reduce | flops 2 | bytes 16 | tf_op jit(solution)/shard_map/psum | solution.py:156
  (1034 shorter events, 477.9 us)
Async XLA Ops:
  17.0 17.1 %collective-permute-start.2 = (f32[11,256]{0,1:T(8,128)S(1)}, f32[11,256]{0,1:T(8,128)S(1)}, u32[]{:S(2)}, u32[]{:S(2)}) collective-permute-start(f32[11,256]{0,1:T(8,128)S(1)} %multiply_bitcast_fusion.27), channel_id=1, source_target_pairs={{0,16},{16,0},{4,20},{20,4},{8,24},{24,8},{12,28},{28,12},{32,48},... | collective-permute-start | bytes 33800 | tf_op jit(solution)/shard_map/ppermute | solution.py:27
  27.3 15.4 %collective-permute-start.3 = (f32[1,11,512]{1,2,0:T(8,128)}, f32[1,11,512]{1,2,0:T(8,128)S(1)}, u32[]{:S(2)}, u32[]{:S(2)}) collective-permute-start(f32[1,11,512]{1,2,0:T(8,128)} %bitcast.30), channel_id=1, source_target_pairs={{0,1},{1,2},{2,3},{4,5},{5,6},{6,7},{8,9},{9,10},{10,11},{12,13},{... | collective-permute-start | bytes 67592 | tf_op jit(solution)/shard_map/ppermute | solution.py:35
  31.6 15.1 %collective-permute-start.4 = (f32[1,11,512]{1,2,0:T(8,128)S(1)}, f32[1,11,512]{1,2,0:T(8,128)S(1)}, u32[]{:S(2)}, u32[]{:S(2)}) collective-permute-start(f32[1,11,512]{1,2,0:T(8,128)S(1)} %bitcast.841), channel_id=1, source_target_pairs={{1,0},{2,1},{3,2},{5,4},{6,5},{7,6},{9,8},{10,9},{11,10},{13,12},{... | collective-permute-start | bytes 67592 | tf_op jit(solution)/shard_map/ppermute | solution.py:38
  172.3 18.5 %collective-permute-start.7 = (f32[2,256]{0,1:T(8,128)S(1)}, f32[2,256]{0,1:T(8,128)S(1)}, u32[]{:S(2)}, u32[]{:S(2)}) collective-permute-start(f32[2,256]{0,1:T(8,128)S(1)} %multiply_bitcast_fusion.24), channel_id=1, source_target_pairs={{0,16},{16,0},{4,20},{20,4},{8,24},{24,8},{12,28},{28,12},{32,48},... | collective-permute-start | bytes 6152 | tf_op jit(solution)/shard_map/ppermute | solution.py:27
  177.6 17.3 %collective-permute-start.6 = (f32[2,256]{0,1:T(8,128)S(1)}, f32[2,256]{0,1:T(8,128)S(1)}, u32[]{:S(2)}, u32[]{:S(2)}) collective-permute-start(f32[2,256]{0,1:T(8,128)S(1)} %multiply_bitcast_fusion.25), channel_id=1, source_target_pairs={{0,8},{8,0},{4,12},{12,4},{16,24},{24,16},{20,28},{28,20},{32,40},... | collective-permute-start | bytes 6152 | tf_op jit(solution)/shard_map/ppermute | solution.py:27
  181.1 15.1 %collective-permute-start.5 = (f32[2,256]{0,1:T(8,128)S(1)}, f32[2,256]{0,1:T(8,128)S(1)}, u32[]{:S(2)}, u32[]{:S(2)}) collective-permute-start(f32[2,256]{0,1:T(8,128)S(1)} %multiply_bitcast_fusion.26), channel_id=1, source_target_pairs={{0,4},{4,0},{8,12},{12,8},{16,20},{20,16},{24,28},{28,24},{32,36},... | collective-permute-start | bytes 6152 | tf_op jit(solution)/shard_map/ppermute | solution.py:27
  182.2 29.1 %collective-permute-start.8 = (f32[1,2,512]{1,2,0:T(8,128)}, f32[1,2,512]{1,2,0:T(8,128)S(1)}, u32[]{:S(2)}, u32[]{:S(2)}) collective-permute-start(f32[1,2,512]{1,2,0:T(8,128)} %bitcast.54), channel_id=1, source_target_pairs={{0,1},{1,2},{2,3},{4,5},{5,6},{6,7},{8,9},{9,10},{10,11},{12,13},{... | collective-permute-start | bytes 12296 | tf_op jit(solution)/shard_map/ppermute | solution.py:35
  183.5 31.9 %collective-permute-start.9 = (f32[1,2,512]{1,2,0:T(8,128)}, f32[1,2,512]{1,2,0:T(8,128)S(1)}, u32[]{:S(2)}, u32[]{:S(2)}) collective-permute-start(f32[1,2,512]{1,2,0:T(8,128)} %bitcast.878), channel_id=1, source_target_pairs={{1,0},{2,1},{3,2},{5,4},{6,5},{7,6},{9,8},{10,9},{11,10},{13,12},{... | collective-permute-start | bytes 12296 | tf_op jit(solution)/shard_map/ppermute | solution.py:38
  247.5 14.0 %collective-permute-start.18 = (f32[1,6,512]{1,2,0:T(8,128)}, f32[1,6,512]{1,2,0:T(8,128)S(1)}, u32[]{:S(2)}, u32[]{:S(2)}) collective-permute-start(f32[1,6,512]{1,2,0:T(8,128)} %bitcast.96), channel_id=1, source_target_pairs={{0,1},{1,2},{2,3},{4,5},{5,6},{6,7},{8,9},{9,10},{10,11},{12,13},{... | collective-permute-start | bytes 36872 | tf_op jit(solution)/shard_map/ppermute | solution.py:35
  302.9 14.1 %collective-permute-start.23 = (f32[1,8,512]{1,2,0:T(8,128)}, f32[1,8,512]{1,2,0:T(8,128)S(1)}, u32[]{:S(2)}, u32[]{:S(2)}) collective-permute-start(f32[1,8,512]{1,2,0:T(8,128)} %bitcast.125), channel_id=1, source_target_pairs={{0,1},{1,2},{2,3},{4,5},{5,6},{6,7},{8,9},{9,10},{10,11},{12,13},{... | collective-permute-start | bytes 49160 | tf_op jit(solution)/shard_map/ppermute | solution.py:35
  307.2 13.9 %collective-permute-start.24 = (f32[1,8,512]{1,2,0:T(8,128)}, f32[1,8,512]{1,2,0:T(8,128)S(1)}, u32[]{:S(2)}, u32[]{:S(2)}) collective-permute-start(f32[1,8,512]{1,2,0:T(8,128)} %bitcast.870), channel_id=1, source_target_pairs={{1,0},{2,1},{3,2},{5,4},{6,5},{7,6},{9,8},{10,9},{11,10},{13,12},{... | collective-permute-start | bytes 49160 | tf_op jit(solution)/shard_map/ppermute | solution.py:38
  493.0 14.0 %collective-permute-start.29 = (f32[1,2,512]{1,2,0:T(8,128)}, f32[1,2,512]{1,2,0:T(8,128)S(1)}, u32[]{:S(2)}, u32[]{:S(2)}) collective-permute-start(f32[1,2,512]{1,2,0:T(8,128)} %bitcast.880), channel_id=1, source_target_pairs={{1,0},{2,1},{3,2},{5,4},{6,5},{7,6},{9,8},{10,9},{11,10},{13,12},{... | collective-permute-start | bytes 12296 | tf_op jit(solution)/shard_map/ppermute | solution.py:38
  540.7 14.1 %collective-permute-start.33 = (f32[1,6,512]{1,2,0:T(8,128)}, f32[1,6,512]{1,2,0:T(8,128)S(1)}, u32[]{:S(2)}, u32[]{:S(2)}) collective-permute-start(f32[1,6,512]{1,2,0:T(8,128)} %bitcast.177), channel_id=1, source_target_pairs={{0,1},{1,2},{2,3},{4,5},{5,6},{6,7},{8,9},{9,10},{10,11},{12,13},{... | collective-permute-start | bytes 36872 | tf_op jit(solution)/shard_map/ppermute | solution.py:35
  545.0 13.8 %collective-permute-start.34 = (f32[1,6,512]{1,2,0:T(8,128)}, f32[1,6,512]{1,2,0:T(8,128)S(1)}, u32[]{:S(2)}, u32[]{:S(2)}) collective-permute-start(f32[1,6,512]{1,2,0:T(8,128)} %bitcast.868), channel_id=1, source_target_pairs={{1,0},{2,1},{3,2},{5,4},{6,5},{7,6},{9,8},{10,9},{11,10},{13,12},{... | collective-permute-start | bytes 36872 | tf_op jit(solution)/shard_map/ppermute | solution.py:38
  596.0 15.0 %collective-permute-start.38 = (f32[1,8,512]{1,2,0:T(8,128)}, f32[1,8,512]{1,2,0:T(8,128)S(1)}, u32[]{:S(2)}, u32[]{:S(2)}) collective-permute-start(f32[1,8,512]{1,2,0:T(8,128)} %bitcast.203), channel_id=1, source_target_pairs={{0,1},{1,2},{2,3},{4,5},{5,6},{6,7},{8,9},{9,10},{10,11},{12,13},{... | collective-permute-start | bytes 49160 | tf_op jit(solution)/shard_map/ppermute | solution.py:35
  600.3 14.8 %collective-permute-start.39 = (f32[1,8,512]{1,2,0:T(8,128)}, f32[1,8,512]{1,2,0:T(8,128)S(1)}, u32[]{:S(2)}, u32[]{:S(2)}) collective-permute-start(f32[1,8,512]{1,2,0:T(8,128)} %bitcast.871), channel_id=1, source_target_pairs={{1,0},{2,1},{3,2},{5,4},{6,5},{7,6},{9,8},{10,9},{11,10},{13,12},{... | collective-permute-start | bytes 49160 | tf_op jit(solution)/shard_map/ppermute | solution.py:38
  790.0 14.8 %collective-permute-start.44 = (f32[1,2,512]{1,2,0:T(8,128)}, f32[1,2,512]{1,2,0:T(8,128)S(1)}, u32[]{:S(2)}, u32[]{:S(2)}) collective-permute-start(f32[1,2,512]{1,2,0:T(8,128)} %bitcast.879), channel_id=1, source_target_pairs={{1,0},{2,1},{3,2},{5,4},{6,5},{7,6},{9,8},{10,9},{11,10},{13,12},{... | collective-permute-start | bytes 12296 | tf_op jit(solution)/shard_map/ppermute | solution.py:38
  837.8 15.6 %collective-permute-start.48 = (f32[1,6,512]{1,2,0:T(8,128)}, f32[1,6,512]{1,2,0:T(8,128)S(1)}, u32[]{:S(2)}, u32[]{:S(2)}) collective-permute-start(f32[1,6,512]{1,2,0:T(8,128)} %bitcast.258), channel_id=1, source_target_pairs={{0,1},{1,2},{2,3},{4,5},{5,6},{6,7},{8,9},{9,10},{10,11},{12,13},{... | collective-permute-start | bytes 36872 | tf_op jit(solution)/shard_map/ppermute | solution.py:35
  842.1 15.3 %collective-permute-start.49 = (f32[1,6,512]{1,2,0:T(8,128)}, f32[1,6,512]{1,2,0:T(8,128)S(1)}, u32[]{:S(2)}, u32[]{:S(2)}) collective-permute-start(f32[1,6,512]{1,2,0:T(8,128)} %bitcast.869), channel_id=1, source_target_pairs={{1,0},{2,1},{3,2},{5,4},{6,5},{7,6},{9,8},{10,9},{11,10},{13,12},{... | collective-permute-start | bytes 36872 | tf_op jit(solution)/shard_map/ppermute | solution.py:38
  887.2 16.7 %collective-permute-start.52 = (f32[8,256]{0,1:T(8,128)S(1)}, f32[8,256]{0,1:T(8,128)}, u32[]{:S(2)}, u32[]{:S(2)}) collective-permute-start(f32[8,256]{0,1:T(8,128)S(1)} %multiply_bitcast_fusion), channel_id=1, source_target_pairs={{0,16},{16,0},{4,20},{20,4},{8,24},{24,8},{12,28},{28,12},{32,48},... | collective-permute-start | bytes 24584 | tf_op jit(solution)/shard_map/ppermute | solution.py:27
  888.9 15.9 %collective-permute-start.51 = (f32[8,256]{0,1:T(8,128)}, f32[8,256]{0,1:T(8,128)}, u32[]{:S(2)}, u32[]{:S(2)}) collective-permute-start(f32[8,256]{0,1:T(8,128)} %multiply_bitcast_fusion.1), channel_id=1, source_target_pairs={{0,8},{8,0},{4,12},{12,4},{16,24},{24,16},{20,28},{28,20},{32,40},... | collective-permute-start | bytes 24584 | tf_op jit(solution)/shard_map/ppermute | solution.py:27
  891.4 14.5 %collective-permute-start.50 = (f32[8,256]{0,1:T(8,128)}, f32[8,256]{0,1:T(8,128)}, u32[]{:S(2)}, u32[]{:S(2)}) collective-permute-start(f32[8,256]{0,1:T(8,128)} %multiply_bitcast_fusion.2), channel_id=1, source_target_pairs={{0,4},{4,0},{8,12},{12,8},{16,20},{20,16},{24,28},{28,24},{32,36},... | collective-permute-start | bytes 24584 | tf_op jit(solution)/shard_map/ppermute | solution.py:27
  898.0 16.9 %collective-permute-start.53 = (f32[1,8,512]{1,2,0:T(8,128)}, f32[1,8,512]{1,2,0:T(8,128)S(1)}, u32[]{:S(2)}, u32[]{:S(2)}) collective-permute-start(f32[1,8,512]{1,2,0:T(8,128)} %bitcast.284), channel_id=1, source_target_pairs={{0,1},{1,2},{2,3},{4,5},{5,6},{6,7},{8,9},{9,10},{10,11},{12,13},{... | collective-permute-start | bytes 49160 | tf_op jit(solution)/shard_map/ppermute | solution.py:35
  902.3 16.7 %collective-permute-start.54 = (f32[1,8,512]{1,2,0:T(8,128)}, f32[1,8,512]{1,2,0:T(8,128)S(1)}, u32[]{:S(2)}, u32[]{:S(2)}) collective-permute-start(f32[1,8,512]{1,2,0:T(8,128)} %bitcast.866), channel_id=1, source_target_pairs={{1,0},{2,1},{3,2},{5,4},{6,5},{7,6},{9,8},{10,9},{11,10},{13,12},{... | collective-permute-start | bytes 49160 | tf_op jit(solution)/shard_map/ppermute | solution.py:38
  (143 other events, 3113.8 us)
where the time goes:
time: 1090 us; the launch traced here: 1080 us
  blocking collectives  526 us (48%)
  other arithmetic  226 us (21%)
  local copies, waits for them, and re-layouts  218 us (20%)
  starting transfers between devices  93.7 us (9%)
    psum x4, blocking collectives, weighted_norms(): lax.psum(jnp.sum(weights * vectors * vectors, axis=(1, 2)), ('sub', 'slab'))  301 us
    psum x3, blocking collectives, per_device(): heights = lax.psum(local_heights, ('sub', 'slab'))  224 us
    scatter-add x33, other arithmetic, assemble(): summed = summed.at[:, iface_nodes[matching]].add(incoming[matching])  82.6 us
    another operation x136, local copies, waits for them, and re-layouts, node_sums(): corner_block = element_out[:, corner].reshape(channels, EX, EY, EZ)  72.7 us
    scatter-add x11, other arithmetic, assemble(): return summed.at[:, face_nodes[1]].add(extended[3])  44.3 us
    scatter-add x11, other arithmetic, assemble(): summed = summed.at[:, face_nodes[0]].add(extended[0])  44.3 us
    ppermute x11, starting transfers between devices, extended_2(): lax.ppermute(lax.slice_in_dim(block, block.shape[dim] - width, None, axis...  39.7 us
    ppermute x33, starting transfers between devices, swapped(): return lax.ppermute(block, axis, route)  39.5 us
  transfers between devices with their start and end apart: 55, of which 1 were waited for; matrix products, arithmetic and copies ran while one was open for 17% of the time, Pallas kernels for 0%

commit v1 on v0

--- a/solution.py
+++ b/solution.py
@@ -2,6 +2,7 @@
 import jax.numpy as jnp
 from jax import lax
 from jax.sharding import PartitionSpec as P
+from jax.lax import psum
 
 EX = 4
 EY = 4
@@ -153,7 +154,13 @@
 
 
 def weighted_norms(vectors, weights):
-    return lax.psum(jnp.sum(weights * vectors * vectors, axis=(1, 2)), ("sub", "slab"))
+
+    def divide_lines(original, along_axis, link_axis="slab"):
+        t_next = psum(original, along_axis)
+        lower = psum(t_next, link_axis)
+        return lower
+
+    return divide_lines(jnp.sum(weights * vectors * vectors, axis=(1, 2)), "sub")
 
 
 def triangular_solves(factor, target):

time: 1090 us -> 1330 us (1.22)
  blocking collectives: 526 us -> 756 us
    psum x4 -> x8, blocking collectives: 301 us -> 531 us  [the longest x4 496 us: divide_lines(): t_next = psum(original, along_axis)]
  transfers between devices with their start and end apart: 55 -> 55, of which waited for: 1 -> 0; matrix products, arithmetic and copies ran while one was open for 17% -> 14% of each run, Pallas kernels for 0% -> 0%
where the time goes in v1:
time: 1330 us; the launch traced here: 1320 us
  blocking collectives  756 us (57%)
  other arithmetic  226 us (17%)
  local copies, waits for them, and re-layouts  217 us (16%)
  starting transfers between devices  100 us (8%)
    psum x4, blocking collectives, divide_lines(): t_next = psum(original, along_axis)  496 us
    psum x3, blocking collectives, per_device(): heights = lax.psum(local_heights, ('sub', 'slab'))  226 us
    scatter-add x33, other arithmetic, assemble(): summed = summed.at[:, iface_nodes[matching]].add(incoming[matching])  83 us
    another operation x136, local copies, waits for them, and re-layouts, node_sums(): corner_block = element_out[:, corner].reshape(channels, EX, EY, EZ)  72.7 us
    ppermute x33, starting transfers between devices, swapped(): return lax.ppermute(block, axis, route)  46.1 us
    scatter-add x11, other arithmetic, assemble(): return summed.at[:, face_nodes[1]].add(extended[3])  44.9 us
    scatter-add x11, other arithmetic, assemble(): summed = summed.at[:, face_nodes[0]].add(extended[0])  43.7 us
    ppermute x11, starting transfers between devices, extended_2(): lax.ppermute(lax.slice_in_dim(block, block.shape[dim] - width, None, axis...  39.7 us
  transfers between devices with their start and end apart: 55, of which 0 were waited for; matrix products, arithmetic and copies ran while one was open for 14% of the time, Pallas kernels for 0%

profile of v1, /device:TPU:1, one launch (start us, length us, event | category | flops | bytes accessed | tf_op | source)
XLA Modules:
  0.0 1315.5 jit_solution(14887674441806735688)
XLA Ops:
  51.5 124.1 %psum.77 = f32[2]{0:T(128)S(1)} all-reduce(f32[2]{0:T(128)S(1)} %reduce_sum.120), channel_id=1, replica_groups=mesh['sub'=64,'slab'=4] {'sub'}, use_global_device_ids=true, to_apply=%region_11.12 | all-reduce | flops 2 | bytes 16 | tf_op jit(solution)/shard_map/psum | solution.py:159
  176.1 10.2 psum.78
  230.2 7.7 collective-permute-start.10
  269.8 4.1 scatter_custom_fusion.12
  306.0 4.3 collective-permute-start.18
  324.1 4.2 scatter_custom_fusion.23
  362.2 4.3 collective-permute-start.23
  385.3 74.4 %psum.79 = f32[2,1]{0,1:T(1,128)S(1)} all-reduce(f32[2,1]{0,1:T(1,128)S(1)} %bitcast.878), channel_id=1, replica_groups=mesh['sub'=64,'slab'=4] {'sub','slab'}, use_global_device_ids=true, to_apply=%region_35.36 | all-reduce | flops 2 | bytes 16 | tf_op jit(solution)/shard_map/psum | solution.py:243
  460.3 124.1 %psum.80 = f32[2]{0:T(128)S(1)} all-reduce(f32[2]{0:T(128)S(1)} %reduce_sum.129), channel_id=1, replica_groups=mesh['sub'=64,'slab'=4] {'sub'}, use_global_device_ids=true, to_apply=%region_38.39 | all-reduce | flops 2 | bytes 16 | tf_op jit(solution)/shard_map/psum | solution.py:159
  584.5 7.6 psum.81
  625.0 4.2 scatter_custom_fusion.33
  660.4 4.3 collective-permute-start.33
  678.8 4.4 scatter_custom_fusion.38
  714.2 4.3 collective-permute-start.38
  738.6 75.6 %psum.82 = f32[2,2]{0,1:T(2,128)S(1)} all-reduce(f32[2,2]{0,1:T(2,128)S(1)} %pad_maximum_fusion.8), channel_id=1, replica_groups=mesh['sub'=64,'slab'=4] {'sub','slab'}, use_global_device_ids=true, to_apply=%region_59.60 | all-reduce | flops 4 | bytes 32 | tf_op jit(solution)/shard_map/psum | solution.py:243
  815.4 124.1 %psum.83 = f32[2]{0:T(128)S(1)} all-reduce(f32[2]{0:T(128)S(1)} %reduce_sum.144), channel_id=1, replica_groups=mesh['sub'=64,'slab'=4] {'sub'}, use_global_device_ids=true, to_apply=%region_62.63 | all-reduce | flops 2 | bytes 16 | tf_op jit(solution)/shard_map/psum | solution.py:159
  939.5 8.3 psum.84
  980.6 4.4 scatter_custom_fusion.48
  1016.9 4.3 collective-permute-start.48
  1036.7 4.3 scatter_custom_fusion.53
  1074.1 4.3 collective-permute-start.53
  1099.7 75.6 %psum.85 = f32[2,3]{0,1:T(4,128)S(1)} all-reduce(f32[2,3]{0,1:T(4,128)S(1)} %pad_maximum_fusion.7), channel_id=1, replica_groups=mesh['sub'=64,'slab'=4] {'sub','slab'}, use_global_device_ids=true, to_apply=%region_86.87 | all-reduce | flops 6 | bytes 48 | tf_op jit(solution)/shard_map/psum | solution.py:243
  1176.3 124.1 %psum.86 = f32[2]{0:T(128)S(1)} all-reduce(f32[2]{0:T(128)S(1)} %reduce_sum.189), channel_id=1, replica_groups=mesh['sub'=64,'slab'=4] {'sub'}, use_global_device_ids=true, to_apply=%region_89.90 | all-reduce | flops 2 | bytes 16 | tf_op jit(solution)/shard_map/psum | solution.py:159
  1303.6 8.1 psum.87
  (1038 shorter events, 494.4 us)
Async XLA Ops:
  17.0 17.1 %collective-permute-start.2 = (f32[11,256]{0,1:T(8,128)S(1)}, f32[11,256]{0,1:T(8,128)S(1)}, u32[]{:S(2)}, u32[]{:S(2)}) collective-permute-start(f32[11,256]{0,1:T(8,128)S(1)} %multiply_bitcast_fusion.27), channel_id=1, source_target_pairs={{0,16},{16,0},{4,20},{20,4},{8,24},{24,8},{12,28},{28,12},{32,48},... | collective-permute-start | bytes 33800 | tf_op jit(solution)/shard_map/ppermute | solution.py:28
  27.3 15.4 %collective-permute-start.3 = (f32[1,11,512]{1,2,0:T(8,128)}, f32[1,11,512]{1,2,0:T(8,128)S(1)}, u32[]{:S(2)}, u32[]{:S(2)}) collective-permute-start(f32[1,11,512]{1,2,0:T(8,128)} %bitcast.30), channel_id=1, source_target_pairs={{0,1},{1,2},{2,3},{4,5},{5,6},{6,7},{8,9},{9,10},{10,11},{12,13},{... | collective-permute-start | bytes 67592 | tf_op jit(solution)/shard_map/ppermute | solution.py:36
  31.6 15.1 %collective-permute-start.4 = (f32[1,11,512]{1,2,0:T(8,128)S(1)}, f32[1,11,512]{1,2,0:T(8,128)S(1)}, u32[]{:S(2)}, u32[]{:S(2)}) collective-permute-start(f32[1,11,512]{1,2,0:T(8,128)S(1)} %bitcast.842), channel_id=1, source_target_pairs={{1,0},{2,1},{3,2},{5,4},{6,5},{7,6},{9,8},{10,9},{11,10},{13,12},{... | collective-permute-start | bytes 67592 | tf_op jit(solution)/shard_map/ppermute | solution.py:39
  227.5 21.8 %collective-permute-start.7 = (f32[2,256]{0,1:T(8,128)S(1)}, f32[2,256]{0,1:T(8,128)S(1)}, u32[]{:S(2)}, u32[]{:S(2)}) collective-permute-start(f32[2,256]{0,1:T(8,128)S(1)} %multiply_bitcast_fusion.24), channel_id=1, source_target_pairs={{0,16},{16,0},{4,20},{20,4},{8,24},{24,8},{12,28},{28,12},{32,48},... | collective-permute-start | bytes 6152 | tf_op jit(solution)/shard_map/ppermute | solution.py:28
  238.0 15.4 %collective-permute-start.6 = (f32[2,256]{0,1:T(8,128)S(1)}, f32[2,256]{0,1:T(8,128)S(1)}, u32[]{:S(2)}, u32[]{:S(2)}) collective-permute-start(f32[2,256]{0,1:T(8,128)S(1)} %multiply_bitcast_fusion.25), channel_id=1, source_target_pairs={{0,8},{8,0},{4,12},{12,4},{16,24},{24,16},{20,28},{28,20},{32,40},... | collective-permute-start | bytes 6152 | tf_op jit(solution)/shard_map/ppermute | solution.py:28
  240.0 14.7 %collective-permute-start.5 = (f32[2,256]{0,1:T(8,128)S(1)}, f32[2,256]{0,1:T(8,128)S(1)}, u32[]{:S(2)}, u32[]{:S(2)}) collective-permute-start(f32[2,256]{0,1:T(8,128)S(1)} %multiply_bitcast_fusion.26), channel_id=1, source_target_pairs={{0,4},{4,0},{8,12},{12,8},{16,20},{20,16},{24,28},{28,24},{32,36},... | collective-permute-start | bytes 6152 | tf_op jit(solution)/shard_map/ppermute | solution.py:28
  240.7 29.1 %collective-permute-start.8 = (f32[1,2,512]{1,2,0:T(8,128)}, f32[1,2,512]{1,2,0:T(8,128)S(1)}, u32[]{:S(2)}, u32[]{:S(2)}) collective-permute-start(f32[1,2,512]{1,2,0:T(8,128)} %bitcast.54), channel_id=1, source_target_pairs={{0,1},{1,2},{2,3},{4,5},{5,6},{6,7},{8,9},{9,10},{10,11},{12,13},{... | collective-permute-start | bytes 12296 | tf_op jit(solution)/shard_map/ppermute | solution.py:36
  242.0 31.9 %collective-permute-start.9 = (f32[1,2,512]{1,2,0:T(8,128)}, f32[1,2,512]{1,2,0:T(8,128)S(1)}, u32[]{:S(2)}, u32[]{:S(2)}) collective-permute-start(f32[1,2,512]{1,2,0:T(8,128)} %bitcast.879), channel_id=1, source_target_pairs={{1,0},{2,1},{3,2},{5,4},{6,5},{7,6},{9,8},{10,9},{11,10},{13,12},{... | collective-permute-start | bytes 12296 | tf_op jit(solution)/shard_map/ppermute | solution.py:39
  306.0 14.0 %collective-permute-start.18 = (f32[1,6,512]{1,2,0:T(8,128)}, f32[1,6,512]{1,2,0:T(8,128)S(1)}, u32[]{:S(2)}, u32[]{:S(2)}) collective-permute-start(f32[1,6,512]{1,2,0:T(8,128)} %bitcast.96), channel_id=1, source_target_pairs={{0,1},{1,2},{2,3},{4,5},{5,6},{6,7},{8,9},{9,10},{10,11},{12,13},{... | collective-permute-start | bytes 36872 | tf_op jit(solution)/shard_map/ppermute | solution.py:36
  310.3 13.8 %collective-permute-start.19 = (f32[1,6,512]{1,2,0:T(8,128)}, f32[1,6,512]{1,2,0:T(8,128)S(1)}, u32[]{:S(2)}, u32[]{:S(2)}) collective-permute-start(f32[1,6,512]{1,2,0:T(8,128)} %bitcast.868), channel_id=1, source_target_pairs={{1,0},{2,1},{3,2},{5,4},{6,5},{7,6},{9,8},{10,9},{11,10},{13,12},{... | collective-permute-start | bytes 36872 | tf_op jit(solution)/shard_map/ppermute | solution.py:39
  353.9 13.8 %collective-permute-start.22 = (f32[8,256]{0,1:T(8,128)S(1)}, f32[8,256]{0,1:T(8,128)S(1)}, u32[]{:S(2)}, u32[]{:S(2)}) collective-permute-start(f32[8,256]{0,1:T(8,128)S(1)} %multiply_bitcast_fusion.18), channel_id=1, source_target_pairs={{0,16},{16,0},{4,20},{20,4},{8,24},{24,8},{12,28},{28,12},{32,48},... | collective-permute-start | bytes 24584 | tf_op jit(solution)/shard_map/ppermute | solution.py:28
  362.2 14.1 %collective-permute-start.23 = (f32[1,8,512]{1,2,0:T(8,128)}, f32[1,8,512]{1,2,0:T(8,128)S(1)}, u32[]{:S(2)}, u32[]{:S(2)}) collective-permute-start(f32[1,8,512]{1,2,0:T(8,128)} %bitcast.125), channel_id=1, source_target_pairs={{0,1},{1,2},{2,3},{4,5},{5,6},{6,7},{8,9},{9,10},{10,11},{12,13},{... | collective-permute-start | bytes 49160 | tf_op jit(solution)/shard_map/ppermute | solution.py:36
  366.4 13.9 %collective-permute-start.24 = (f32[1,8,512]{1,2,0:T(8,128)}, f32[1,8,512]{1,2,0:T(8,128)S(1)}, u32[]{:S(2)}, u32[]{:S(2)}) collective-permute-start(f32[1,8,512]{1,2,0:T(8,128)} %bitcast.871), channel_id=1, source_target_pairs={{1,0},{2,1},{3,2},{5,4},{6,5},{7,6},{9,8},{10,9},{11,10},{13,12},{... | collective-permute-start | bytes 49160 | tf_op jit(solution)/shard_map/ppermute | solution.py:39
  650.9 15.1 %collective-permute-start.32 = (f32[6,256]{0,1:T(8,128)S(1)}, f32[6,256]{0,1:T(8,128)S(1)}, u32[]{:S(2)}, u32[]{:S(2)}) collective-permute-start(f32[6,256]{0,1:T(8,128)S(1)} %multiply_bitcast_fusion.12), channel_id=1, source_target_pairs={{0,16},{16,0},{4,20},{20,4},{8,24},{24,8},{12,28},{28,12},{32,48},... | collective-permute-start | bytes 18440 | tf_op jit(solution)/shard_map/ppermute | solution.py:28
  660.4 14.3 %collective-permute-start.33 = (f32[1,6,512]{1,2,0:T(8,128)}, f32[1,6,512]{1,2,0:T(8,128)S(1)}, u32[]{:S(2)}, u32[]{:S(2)}) collective-permute-start(f32[1,6,512]{1,2,0:T(8,128)} %bitcast.177), channel_id=1, source_target_pairs={{0,1},{1,2},{2,3},{4,5},{5,6},{6,7},{8,9},{9,10},{10,11},{12,13},{... | collective-permute-start | bytes 36872 | tf_op jit(solution)/shard_map/ppermute | solution.py:36
  664.7 14.1 %collective-permute-start.34 = (f32[1,6,512]{1,2,0:T(8,128)}, f32[1,6,512]{1,2,0:T(8,128)S(1)}, u32[]{:S(2)}, u32[]{:S(2)}) collective-permute-start(f32[1,6,512]{1,2,0:T(8,128)} %bitcast.869), channel_id=1, source_target_pairs={{1,0},{2,1},{3,2},{5,4},{6,5},{7,6},{9,8},{10,9},{11,10},{13,12},{... | collective-permute-start | bytes 36872 | tf_op jit(solution)/shard_map/ppermute | solution.py:39
  714.2 15.0 %collective-permute-start.38 = (f32[1,8,512]{1,2,0:T(8,128)}, f32[1,8,512]{1,2,0:T(8,128)S(1)}, u32[]{:S(2)}, u32[]{:S(2)}) collective-permute-start(f32[1,8,512]{1,2,0:T(8,128)} %bitcast.203), channel_id=1, source_target_pairs={{0,1},{1,2},{2,3},{4,5},{5,6},{6,7},{8,9},{9,10},{10,11},{12,13},{... | collective-permute-start | bytes 49160 | tf_op jit(solution)/shard_map/ppermute | solution.py:36
  718.5 14.8 %collective-permute-start.39 = (f32[1,8,512]{1,2,0:T(8,128)}, f32[1,8,512]{1,2,0:T(8,128)S(1)}, u32[]{:S(2)}, u32[]{:S(2)}) collective-permute-start(f32[1,8,512]{1,2,0:T(8,128)} %bitcast.872), channel_id=1, source_target_pairs={{1,0},{2,1},{3,2},{5,4},{6,5},{7,6},{9,8},{10,9},{11,10},{13,12},{... | collective-permute-start | bytes 49160 | tf_op jit(solution)/shard_map/ppermute | solution.py:39
  966.2 14.4 %collective-permute-start.44 = (f32[1,2,512]{1,2,0:T(8,128)}, f32[1,2,512]{1,2,0:T(8,128)S(1)}, u32[]{:S(2)}, u32[]{:S(2)}) collective-permute-start(f32[1,2,512]{1,2,0:T(8,128)} %bitcast.880), channel_id=1, source_target_pairs={{1,0},{2,1},{3,2},{5,4},{6,5},{7,6},{9,8},{10,9},{11,10},{13,12},{... | collective-permute-start | bytes 12296 | tf_op jit(solution)/shard_map/ppermute | solution.py:39
  1006.8 16.3 %collective-permute-start.47 = (f32[6,256]{0,1:T(8,128)S(1)}, f32[6,256]{0,1:T(8,128)S(1)}, u32[]{:S(2)}, u32[]{:S(2)}) collective-permute-start(f32[6,256]{0,1:T(8,128)S(1)} %multiply_bitcast_fusion.3), channel_id=1, source_target_pairs={{0,16},{16,0},{4,20},{20,4},{8,24},{24,8},{12,28},{28,12},{32,48},... | collective-permute-start | bytes 18440 | tf_op jit(solution)/shard_map/ppermute | solution.py:28
  1016.9 15.7 %collective-permute-start.48 = (f32[1,6,512]{1,2,0:T(8,128)}, f32[1,6,512]{1,2,0:T(8,128)S(1)}, u32[]{:S(2)}, u32[]{:S(2)}) collective-permute-start(f32[1,6,512]{1,2,0:T(8,128)} %bitcast.258), channel_id=1, source_target_pairs={{0,1},{1,2},{2,3},{4,5},{5,6},{6,7},{8,9},{9,10},{10,11},{12,13},{... | collective-permute-start | bytes 36872 | tf_op jit(solution)/shard_map/ppermute | solution.py:36
  1021.2 15.5 %collective-permute-start.49 = (f32[1,6,512]{1,2,0:T(8,128)}, f32[1,6,512]{1,2,0:T(8,128)S(1)}, u32[]{:S(2)}, u32[]{:S(2)}) collective-permute-start(f32[1,6,512]{1,2,0:T(8,128)} %bitcast.870), channel_id=1, source_target_pairs={{1,0},{2,1},{3,2},{5,4},{6,5},{7,6},{9,8},{10,9},{11,10},{13,12},{... | collective-permute-start | bytes 36872 | tf_op jit(solution)/shard_map/ppermute | solution.py:39
  1074.1 16.0 %collective-permute-start.53 = (f32[1,8,512]{1,2,0:T(8,128)}, f32[1,8,512]{1,2,0:T(8,128)S(1)}, u32[]{:S(2)}, u32[]{:S(2)}) collective-permute-start(f32[1,8,512]{1,2,0:T(8,128)} %bitcast.284), channel_id=1, source_target_pairs={{0,1},{1,2},{2,3},{4,5},{5,6},{6,7},{8,9},{9,10},{10,11},{12,13},{... | collective-permute-start | bytes 49160 | tf_op jit(solution)/shard_map/ppermute | solution.py:36
  1078.4 15.8 %collective-permute-start.54 = (f32[1,8,512]{1,2,0:T(8,128)}, f32[1,8,512]{1,2,0:T(8,128)S(1)}, u32[]{:S(2)}, u32[]{:S(2)}) collective-permute-start(f32[1,8,512]{1,2,0:T(8,128)} %bitcast.867), channel_id=1, source_target_pairs={{1,0},{2,1},{3,2},{5,4},{6,5},{7,6},{9,8},{10,9},{11,10},{13,12},{... | collective-permute-start | bytes 49160 | tf_op jit(solution)/shard_map/ppermute | solution.py:39
  (143 other events, 3637.8 us)
